TPU v7x, 256 devices: a whole 4x4x8 slice. The times are simulated.
256 devices in a mesh: seq: 32 (over x, z), head: 8 (over y, core).
Axes of the slice: x: 4, y: 4, z: 8, core: 2. Of those that a mesh axis runs over, the one named last changes fastest.
Arguments:
- tokens: bfloat16 [16384, 4096], P('seq'), may hold values from -6 to 6
- w_xz: bfloat16 [4096, 2, 4096], P('seq', None, 'head'), may hold values from -0.09375 to 0.09375
- w_bc: bfloat16 [4096, 256], P('seq'), may hold values from -0.09375 to 0.09375
- conv_x: float32 [4, 4096], P(None, 'head'), may hold values from -3 to 3
- conv_bc: float32 [4, 256], replicated, may hold values from -3 to 3
- tail_x: bfloat16 [3, 4096], P(None, 'head'), may hold values from -6 to 6
- tail_bc: bfloat16 [3, 256], replicated, may hold values from -6 to 6
- decay_code: int32 [16384, 64], P('seq', 'head'), may hold values from 0 to 196608, as said below
- skip_gain: float32 [64], P('head'), may hold values from 0.5 to 2
- state_in: float32 [64, 64, 128], P('head'), may hold values from -180 to 180
- norm_gain: float32 [4096], P('head'), may hold values from 0.1 to 1.9
- w_out: bfloat16 [4096, 4096], P('head', 'seq'), may hold values from -0.1875 to 0.1875
Outputs:
- mixed: bfloat16 [16384, 4096], P('seq', 'head')
Inputs may be any that keep to these rules, and one draw needn't show every extreme that they name: `decay_code`: the decay factor of a token and head is exp(-code / 262144).
All inputs are finite; a program needn't handle non-finite values.
Results may differ from a plain program's by a relative error of at most 0.0085.
Values may be sent and summed in bfloat16 or wider, within the bound.
A program may use at most 128 MiB of HBM per device.

v0:
```python
import jax
import jax.numpy as jnp
from jax import lax
from jax.sharding import PartitionSpec as P

Q = 256


def passed_along(value, axis, by):
    size = lax.axis_size(axis)
    pairs = [(i, i + by) for i in range(size) if 0 <= i + by < size]
    return lax.ppermute(value, axis, pairs)


def depthwise(pre, tail, kernel):
    whole = jnp.concatenate([tail, pre], axis=0).astype(jnp.float32)
    length = pre.shape[0]
    total = jnp.zeros((length, pre.shape[1]), jnp.float32)
    for offset in range(kernel.shape[0]):
        total = total + kernel[offset] * whole[offset : offset + length]
    return jax.nn.silu(total).astype(jnp.bfloat16)


def block_step(state, inputs):
    xval, bval, cval, logdec = inputs
    cum = jnp.cumsum(logdec, axis=0)
    span = cum.shape[0]
    places = jnp.arange(span)
    lower = places[:, None] >= places[None, :]
    cumt = cum.T
    diff = cumt[:, :, None] - cumt[:, None, :]
    decay = jnp.where(lower[None], jnp.exp(jnp.where(lower[None], diff, 0.0)), 0.0)
    scores = jnp.dot(cval, bval.T, preferred_element_type=jnp.float32)
    weights = (decay * scores[None]).astype(jnp.bfloat16)
    inner = jnp.einsum("hts,shp->thp", weights, xval, preferred_element_type=jnp.float32)
    carried = jnp.einsum(
        "tn,hpn->thp", cval.astype(jnp.float32), state, precision=lax.Precision.HIGHEST
    )
    carried = carried * jnp.exp(cum)[:, :, None]
    tail_decay = jnp.exp(cum[-1][None, :] - cum)
    decayed_b = (tail_decay.T[:, :, None] * bval.astype(jnp.float32)[None]).astype(jnp.bfloat16)
    added = jnp.einsum("hsn,shp->hpn", decayed_b, xval, preferred_element_type=jnp.float32)
    new_state = jnp.exp(cum[-1])[:, None, None] * state + added
    return (new_state, inner + carried)


def local(
    tokens,
    w_xz,
    w_bc,
    conv_x,
    conv_bc,
    tail_x,
    tail_bc,
    decay_code,
    skip_gain,
    state_in,
    norm_gain,
    w_out,
):
    rows = tokens.shape[0]
    heads, head_dim, nstate = state_in.shape
    inner = heads * head_dim
    seq_count = lax.axis_size("seq")
    first = lax.axis_index("seq") == 0
    pieces = (
        lax.all_gather(w_xz, "seq", axis=0, tiled=True),
        lax.all_gather(w_bc, "seq", axis=0, tiled=True),
    )
    count = pieces[0].shape[0]
    xz = jnp.dot(tokens, pieces[0].reshape(count, 2 * inner), preferred_element_type=jnp.float32)
    bc_sum = jnp.dot(tokens, pieces[1], preferred_element_type=jnp.float32)
    x_pre = xz[:, :inner].astype(jnp.bfloat16)
    z_val = xz[:, inner:].astype(jnp.bfloat16)
    bc_pre = bc_sum.astype(jnp.bfloat16)
    lag = conv_x.shape[0] - 1
    before_x, before_bc = passed_along((x_pre[rows - lag :], bc_pre[rows - lag :]), "seq", 1)
    before_x = jnp.where(first, tail_x, before_x)
    before_bc = jnp.where(first, tail_bc, before_bc)
    x_conv = depthwise(x_pre, before_x, conv_x)
    bc_conv = depthwise(bc_pre, before_bc, conv_bc)
    b_val = bc_conv[:, :nstate]
    c_val = bc_conv[:, nstate:]
    logdec = -decay_code.astype(jnp.float32) / (16.0 * rows * seq_count)
    blocks = rows // Q
    inputs = (
        x_conv.reshape(blocks, Q, heads, head_dim),
        b_val.reshape(blocks, Q, nstate),
        c_val.reshape(blocks, Q, nstate),
        logdec.reshape(blocks, Q, heads),
    )
    local_state, parts = lax.scan(block_step, jnp.zeros_like(state_in), inputs)
    parts = parts.reshape(rows, heads, head_dim)
    cum_range = jnp.cumsum(logdec, axis=0)
    range_decay = jnp.exp(cum_range[-1])

    def link(step, incoming):
        outgoing = range_decay[:, None, None] * incoming + local_state
        received = passed_along(outgoing, "seq", 1)
        return jnp.where(first, state_in, received)

    opening = jnp.where(first, state_in, jnp.zeros_like(state_in))
    incoming = lax.fori_loop(0, seq_count - 1, link, opening)
    correction = jnp.einsum(
        "tn,hpn->thp", c_val.astype(jnp.float32), incoming, precision=lax.Precision.HIGHEST
    )
    parts = (parts + correction * jnp.exp(cum_range)[:, :, None]).reshape(rows, inner)
    y_val = parts / nstate + jnp.repeat(skip_gain, head_dim)[None, :] * x_conv.astype(jnp.float32)
    gated = y_val * jax.nn.silu(z_val.astype(jnp.float32))
    total_sq = lax.psum(jnp.sum(gated * gated, axis=1), "head")
    meansq = total_sq / (inner * lax.axis_size("head"))
    normed = (gated * lax.rsqrt(meansq[:, None] + 1e-05) * norm_gain[None, :]).astype(jnp.bfloat16)
    partial_out = jnp.dot(
        normed, lax.all_gather(w_out, "seq", axis=1, tiled=True), preferred_element_type=jnp.float32
    )
    result = lax.psum_scatter(partial_out, "head", scatter_dimension=1, tiled=True)
    return result.astype(jnp.bfloat16)


def solution(mesh):
    return jax.shard_map(
        local,
        mesh=mesh,
        in_specs=(
            P("seq", None),
            P("seq", None, "head"),
            P("seq", None),
            P(None, "head"),
            P(),
            P(None, "head"),
            P(),
            P("seq", "head"),
            P("head"),
            P("head", None, None),
            P("head"),
            P("head", "seq"),
        ),
        out_specs=P("seq", "head"),
        check_vma=False,
    )
```

profile of v0, /device:TPU:1, one launch (start us, length us, event | category | flops | bytes accessed | tf_op | source)
XLA Modules:
  0.0 687.8 jit_solution(6303912154717134488)
XLA Ops:
  13.6 74.2 %all-gather.6.cloned.1.call-done = bf16[4096,256]{1,0:T(8,128)(2,1)} async-done(((bf16[128,256]{1,0:T(8,128)(2,1)}), bf16[4096,256]{1,0:T(8,128)(2,1)}) %all-gather.6.cloned.1.call-update) | async-done | bytes 2097168 | tf_op jit(solution)/shard_map/all_gather | solution.py:68
  95.5 93.9 %all-gather.4.cloned.1.call-done = bf16[4096,2,512]{2,1,0:T(2,128)(2,1)} async-done(((bf16[128,2,512]{2,1,0:T(2,128)(2,1)}), bf16[4096,2,512]{2,1,0:T(2,128)(2,1)}) %all-gather.4.cloned.1.call-update) | async-done | bytes 8388624 | tf_op jit(solution)/shard_map/all_gather | solution.py:67
  189.4 9.3 %copy.40 = bf16[512,8,2,512]{3,1,2,0:T(8,128)(2,1)} copy(bf16[512,8,2,512]{3,2,1,0:T(2,128)(2,1)} %bitcast.88) | data formatting | bytes 16777216
  198.7 9.3 %convolution_convert_fusion = bf16[512,1024]{1,0:T(8,128)(2,1)S(1)} fusion(bf16[512,4096]{1,0:T(8,128)(2,1)} %param.16, bf16[4096,1024]{1,0:T(8,128)(2,1)} %bitcast.89), kind=kOutput, calls=%fused_computation.44 | convolution fusion | flops 4295491584 | bytes 13631488 | tf_op jit(solution)/shard_map/dot_general | solution.py:71
  212.1 30.3 %while.24 = (s32[]{:T(128)}, f32[8,64,128]{2,1,0:T(8,128)S(1)}, f32[2,256,8,64]{1,0,3,2:T(2,128)}, f32[2,256,8]{1,2,0:T(8,128)S(1)}, bf16[2,256,8,64]{1,3,2,0:T(...) while((s32[]{:T(128)}, f32[8,64,128]{2,1,0:T(8,128)S(1)}, ...), condition=%wide.region_3.4_spmd.clone, body=%wide.region_0.3_spmd.clone.sunk | while | flops 322801696 | bytes 6277456 | solution.py:92
  215.2 11.5 %dynamic_update_slice.6 = f32[2,256,8,64]{1,0,3,2:T(2,128)} dynamic-update-slice(f32[2,256,8,64]{1,0,3,2:T(2,128)} %get-tuple-element.276, f32[1,256,8,64]{1,0,3,2:T(1,128)S(1)} %copy.42, s32[]{:T(128)} %get-tuple-element.274, s32[]{:T(128)} %constant.46.clone.1..sunk, s32[]{:T(128)} %constant.46.clone.1..sunk, s32[]{:T(128)} %constant.46.clone.1..sunk) | dynamic-update-slice | bytes 1048580 | tf_op jit(solution)/shard_map/while/body/jit(dynamic_update_index_in_dim)/dynamic_update_slice | solution.py:92
  230.3 11.5 %dynamic_update_slice.6 = f32[2,256,8,64]{1,0,3,2:T(2,128)} dynamic-update-slice(f32[2,256,8,64]{1,0,3,2:T(2,128)} %get-tuple-element.276, f32[1,256,8,64]{1,0,3,2:T(1,128)S(1)} %copy.42, s32[]{:T(128)} %get-tuple-element.274, s32[]{:T(128)} %constant.46.clone.1..sunk, s32[]{:T(128)} %constant.46.clone.1..sunk, s32[]{:T(128)} %constant.46.clone.1..sunk) | dynamic-update-slice | bytes 1048580 | tf_op jit(solution)/shard_map/while/body/jit(dynamic_update_index_in_dim)/dynamic_update_slice | solution.py:92
  244.6 299.9 %while.23 = (s32[]{:T(128)}, f32[8,64,128]{2,1,0:T(8,128)S(1)}, pred[]{:T(512)}, f32[8]{0:T(128)S(1)}, f32[8,64,128]{2,1,0:T(8,128)S(1)}, /*index=5*/f32[8,64,128]{2,1,0:T(8,128)S(1)}, s32[]{:T(128)}) while((s32[]{:T(128)}, f32[8,64,128]{2,1,0:T(8,128)S(1)}, pred[]{:T(512)}, f32[8]{0:T(128)S(1)}, f32[8,64,128]{2,1,0:T(8,128)S(1)}, ...), condition=%wide.region_7.8_spmd, body=%wide.region_6.7_spmd.sunk | while | flops 196610 | bytes 2621590 | solution.py:103
  248.6 8.4 %collective-permute-done = f32[8,64,128]{2,1,0:T(8,128)S(1)} collective-permute-done((f32[8,64,128]{2,1,0:T(8,128)S(1)}, f32[8,64,128]{2,1,0:T(8,128)S(1)}, u32[]{:S(2)}, u32[]{:S(2)}) %collective-permute-start) | collective-permute-done | bytes 262176 | tf_op jit(solution)/shard_map/while/body/eval_jaxpr/ppermute | solution.py:12
  261.3 7.3 %collective-permute-done = f32[8,64,128]{2,1,0:T(8,128)S(1)} collective-permute-done((f32[8,64,128]{2,1,0:T(8,128)S(1)}, f32[8,64,128]{2,1,0:T(8,128)S(1)}, u32[]{:S(2)}, u32[]{:S(2)}) %collective-permute-start) | collective-permute-done | bytes 262176 | tf_op jit(solution)/shard_map/while/body/eval_jaxpr/ppermute | solution.py:12
  314.4 5.8 collective-permute-done
  337.7 6.9 %collective-permute-start = (f32[8,64,128]{2,1,0:T(8,128)S(1)}, f32[8,64,128]{2,1,0:T(8,128)S(1)}, u32[]{:S(2)}, u32[]{:S(2)}) collective-permute-start(f32[8,64,128]{2,1,0:T(8,128)S(1)} %multiply_add_fusion.2), channel_id=1, source_target_pairs={{0,8},{8,16},{16,24},{24,32},{32,40},{40,48},{48,56},{56,64},{64,7... | collective-permute-start | bytes 786440 | tf_op jit(solution)/shard_map/while/body/eval_jaxpr/ppermute | solution.py:12
  411.9 5.9 collective-permute-start
  417.8 5.8 collective-permute-done
  459.3 10.4 %collective-permute-start = (f32[8,64,128]{2,1,0:T(8,128)S(1)}, f32[8,64,128]{2,1,0:T(8,128)S(1)}, u32[]{:S(2)}, u32[]{:S(2)}) collective-permute-start(f32[8,64,128]{2,1,0:T(8,128)S(1)} %multiply_add_fusion.2), channel_id=1, source_target_pairs={{0,8},{8,16},{16,24},{24,32},{32,40},{40,48},{48,56},{56,64},{64,7... | collective-permute-start | bytes 786440 | tf_op jit(solution)/shard_map/while/body/eval_jaxpr/ppermute | solution.py:12
  473.2 5.7 collective-permute-start
  499.8 6.2 collective-permute-start
  509.7 6.2 collective-permute-start
  520.3 6.1 collective-permute-start
  531.5 6.9 collective-permute-start
  538.4 6.1 collective-permute-done
  552.1 45.7 %psum.7 = f32[512]{0:T(512)S(1)} all-reduce(f32[512]{0:T(512)S(1)} %get-tuple-element.160), channel_id=1, replica_groups=mesh['seq'=32,'head'=8] {'head'}, use_global_device_ids=true, to_apply=%region_9.10 | all-reduce | flops 512 | bytes 4096 | tf_op jit(solution)/shard_map/psum | solution.py:110
  597.8 7.8 %fusion.38 = f32[512,4096]{1,0:T(8,128)} fusion(bf16[512,4096]{1,0:T(8,128)(2,1)} %all-gather.8.cloned.1.call-done, f32[512,512]{1,0:T(8,128)S(1)} %get-tuple-element.161, f32[512]{0:T(512)S(1)} %copy-done.3, f32[512]{0:T(512)S(1)} %add_rsqrt_fusion), kind=kOutput, calls=%fused_computation.66 | convolution fusion | flops 2148270080 | bytes 13635584 | tf_op jit(solution)/shard_map/dot_general | solution.py:113
  605.6 73.5 %reduce-scatter.2.cloned.1.call-done = f32[512,512]{1,0:T(8,128)} async-done(((f32[512,4096]{1,0:T(8,128)}), f32[512,512]{1,0:T(8,128)}) %reduce-scatter.2.cloned.1.call-update) | async-done | bytes 1048592 | tf_op jit(solution)/shard_map/reduce_scatter | solution.py:116
  (203 shorter events, 248.8 us)
Async XLA Ops:
  6.5 81.3 %all-gather.6.cloned.1.call-start = ((), (), s32[]{:S(2)}) async-start(), calls=%async_computation.2 | async-start | bytes 2162688 | tf_op jit(solution)/shard_map/all_gather | solution.py:68
  7.3 182.2 %all-gather.4.cloned.1.call-start = ((), (), s32[]{:S(2)}) async-start(), calls=%async_computation.1 | async-start | bytes 8650752 | tf_op jit(solution)/shard_map/all_gather | solution.py:67
  8.0 589.8 %all-gather.8.cloned.1.call-start = ((), (), s32[]{:S(2)}) async-start(), calls=%async_computation.3 | async-start | bytes 4325376 | tf_op jit(solution)/shard_map/all_gather | solution.py:114
  8.7 670.4 %reduce-scatter.2.cloned.1.call-start = ((), (), s32[]{:S(2)}) async-start(), calls=%async_computation.4 | async-start | bytes 9437184 | tf_op jit(solution)/shard_map/reduce_scatter | solution.py:116
  244.7 12.3 %collective-permute-start = (f32[8,64,128]{2,1,0:T(8,128)S(1)}, f32[8,64,128]{2,1,0:T(8,128)S(1)}, u32[]{:S(2)}, u32[]{:S(2)}) collective-permute-start(f32[8,64,128]{2,1,0:T(8,128)S(1)} %multiply_add_fusion.2), channel_id=1, source_target_pairs={{0,8},{8,16},{16,24},{24,32},{32,40},{40,48},{48,56},{56,64},{64,7... | collective-permute-start | bytes 786440 | tf_op jit(solution)/shard_map/while/body/eval_jaxpr/ppermute | solution.py:12
  257.1 11.6 %collective-permute-start = (f32[8,64,128]{2,1,0:T(8,128)S(1)}, f32[8,64,128]{2,1,0:T(8,128)S(1)}, u32[]{:S(2)}, u32[]{:S(2)}) collective-permute-start(f32[8,64,128]{2,1,0:T(8,128)S(1)} %multiply_add_fusion.2), channel_id=1, source_target_pairs={{0,8},{8,16},{16,24},{24,32},{32,40},{40,48},{48,56},{56,64},{64,7... | collective-permute-start | bytes 786440 | tf_op jit(solution)/shard_map/while/body/eval_jaxpr/ppermute | solution.py:12
  268.8 9.0 %collective-permute-start = (f32[8,64,128]{2,1,0:T(8,128)S(1)}, f32[8,64,128]{2,1,0:T(8,128)S(1)}, u32[]{:S(2)}, u32[]{:S(2)}) collective-permute-start(f32[8,64,128]{2,1,0:T(8,128)S(1)} %multiply_add_fusion.2), channel_id=1, source_target_pairs={{0,8},{8,16},{16,24},{24,32},{32,40},{40,48},{48,56},{56,64},{64,7... | collective-permute-start | bytes 786440 | tf_op jit(solution)/shard_map/while/body/eval_jaxpr/ppermute | solution.py:12
  301.3 9.1 %collective-permute-start = (f32[8,64,128]{2,1,0:T(8,128)S(1)}, f32[8,64,128]{2,1,0:T(8,128)S(1)}, u32[]{:S(2)}, u32[]{:S(2)}) collective-permute-start(f32[8,64,128]{2,1,0:T(8,128)S(1)} %multiply_add_fusion.2), channel_id=1, source_target_pairs={{0,8},{8,16},{16,24},{24,32},{32,40},{40,48},{48,56},{56,64},{64,7... | collective-permute-start | bytes 786440 | tf_op jit(solution)/shard_map/while/body/eval_jaxpr/ppermute | solution.py:12
  310.5 9.6 %collective-permute-start = (f32[8,64,128]{2,1,0:T(8,128)S(1)}, f32[8,64,128]{2,1,0:T(8,128)S(1)}, u32[]{:S(2)}, u32[]{:S(2)}) collective-permute-start(f32[8,64,128]{2,1,0:T(8,128)S(1)} %multiply_add_fusion.2), channel_id=1, source_target_pairs={{0,8},{8,16},{16,24},{24,32},{32,40},{40,48},{48,56},{56,64},{64,7... | collective-permute-start | bytes 786440 | tf_op jit(solution)/shard_map/while/body/eval_jaxpr/ppermute | solution.py:12
  320.3 9.0 %collective-permute-start = (f32[8,64,128]{2,1,0:T(8,128)S(1)}, f32[8,64,128]{2,1,0:T(8,128)S(1)}, u32[]{:S(2)}, u32[]{:S(2)}) collective-permute-start(f32[8,64,128]{2,1,0:T(8,128)S(1)} %multiply_add_fusion.2), channel_id=1, source_target_pairs={{0,8},{8,16},{16,24},{24,32},{32,40},{40,48},{48,56},{56,64},{64,7... | collective-permute-start | bytes 786440 | tf_op jit(solution)/shard_map/while/body/eval_jaxpr/ppermute | solution.py:12
  337.7 11.4 %collective-permute-start = (f32[8,64,128]{2,1,0:T(8,128)S(1)}, f32[8,64,128]{2,1,0:T(8,128)S(1)}, u32[]{:S(2)}, u32[]{:S(2)}) collective-permute-start(f32[8,64,128]{2,1,0:T(8,128)S(1)} %multiply_add_fusion.2), channel_id=1, source_target_pairs={{0,8},{8,16},{16,24},{24,32},{32,40},{40,48},{48,56},{56,64},{64,7... | collective-permute-start | bytes 786440 | tf_op jit(solution)/shard_map/while/body/eval_jaxpr/ppermute | solution.py:12
  374.2 8.6 %collective-permute-start = (f32[8,64,128]{2,1,0:T(8,128)S(1)}, f32[8,64,128]{2,1,0:T(8,128)S(1)}, u32[]{:S(2)}, u32[]{:S(2)}) collective-permute-start(f32[8,64,128]{2,1,0:T(8,128)S(1)} %multiply_add_fusion.2), channel_id=1, source_target_pairs={{0,8},{8,16},{16,24},{24,32},{32,40},{40,48},{48,56},{56,64},{64,7... | collective-permute-start | bytes 786440 | tf_op jit(solution)/shard_map/while/body/eval_jaxpr/ppermute | solution.py:12
  391.5 9.3 %collective-permute-start = (f32[8,64,128]{2,1,0:T(8,128)S(1)}, f32[8,64,128]{2,1,0:T(8,128)S(1)}, u32[]{:S(2)}, u32[]{:S(2)}) collective-permute-start(f32[8,64,128]{2,1,0:T(8,128)S(1)} %multiply_add_fusion.2), channel_id=1, source_target_pairs={{0,8},{8,16},{16,24},{24,32},{32,40},{40,48},{48,56},{56,64},{64,7... | collective-permute-start | bytes 786440 | tf_op jit(solution)/shard_map/while/body/eval_jaxpr/ppermute | solution.py:12
  400.9 10.9 %collective-permute-start = (f32[8,64,128]{2,1,0:T(8,128)S(1)}, f32[8,64,128]{2,1,0:T(8,128)S(1)}, u32[]{:S(2)}, u32[]{:S(2)}) collective-permute-start(f32[8,64,128]{2,1,0:T(8,128)S(1)} %multiply_add_fusion.2), channel_id=1, source_target_pairs={{0,8},{8,16},{16,24},{24,32},{32,40},{40,48},{48,56},{56,64},{64,7... | collective-permute-start | bytes 786440 | tf_op jit(solution)/shard_map/while/body/eval_jaxpr/ppermute | solution.py:12
  411.9 11.8 %collective-permute-start = (f32[8,64,128]{2,1,0:T(8,128)S(1)}, f32[8,64,128]{2,1,0:T(8,128)S(1)}, u32[]{:S(2)}, u32[]{:S(2)}) collective-permute-start(f32[8,64,128]{2,1,0:T(8,128)S(1)} %multiply_add_fusion.2), channel_id=1, source_target_pairs={{0,8},{8,16},{16,24},{24,32},{32,40},{40,48},{48,56},{56,64},{64,7... | collective-permute-start | bytes 786440 | tf_op jit(solution)/shard_map/while/body/eval_jaxpr/ppermute | solution.py:12
  423.8 10.4 %collective-permute-start = (f32[8,64,128]{2,1,0:T(8,128)S(1)}, f32[8,64,128]{2,1,0:T(8,128)S(1)}, u32[]{:S(2)}, u32[]{:S(2)}) collective-permute-start(f32[8,64,128]{2,1,0:T(8,128)S(1)} %multiply_add_fusion.2), channel_id=1, source_target_pairs={{0,8},{8,16},{16,24},{24,32},{32,40},{40,48},{48,56},{56,64},{64,7... | collective-permute-start | bytes 786440 | tf_op jit(solution)/shard_map/while/body/eval_jaxpr/ppermute | solution.py:12
  434.4 8.7 %collective-permute-start = (f32[8,64,128]{2,1,0:T(8,128)S(1)}, f32[8,64,128]{2,1,0:T(8,128)S(1)}, u32[]{:S(2)}, u32[]{:S(2)}) collective-permute-start(f32[8,64,128]{2,1,0:T(8,128)S(1)} %multiply_add_fusion.2), channel_id=1, source_target_pairs={{0,8},{8,16},{16,24},{24,32},{32,40},{40,48},{48,56},{56,64},{64,7... | collective-permute-start | bytes 786440 | tf_op jit(solution)/shard_map/while/body/eval_jaxpr/ppermute | solution.py:12
  459.3 13.7 %collective-permute-start = (f32[8,64,128]{2,1,0:T(8,128)S(1)}, f32[8,64,128]{2,1,0:T(8,128)S(1)}, u32[]{:S(2)}, u32[]{:S(2)}) collective-permute-start(f32[8,64,128]{2,1,0:T(8,128)S(1)} %multiply_add_fusion.2), channel_id=1, source_target_pairs={{0,8},{8,16},{16,24},{24,32},{32,40},{40,48},{48,56},{56,64},{64,7... | collective-permute-start | bytes 786440 | tf_op jit(solution)/shard_map/while/body/eval_jaxpr/ppermute | solution.py:12
  473.2 9.0 %collective-permute-start = (f32[8,64,128]{2,1,0:T(8,128)S(1)}, f32[8,64,128]{2,1,0:T(8,128)S(1)}, u32[]{:S(2)}, u32[]{:S(2)}) collective-permute-start(f32[8,64,128]{2,1,0:T(8,128)S(1)} %multiply_add_fusion.2), channel_id=1, source_target_pairs={{0,8},{8,16},{16,24},{24,32},{32,40},{40,48},{48,56},{56,64},{64,7... | collective-permute-start | bytes 786440 | tf_op jit(solution)/shard_map/while/body/eval_jaxpr/ppermute | solution.py:12
  482.3 8.7 %collective-permute-start = (f32[8,64,128]{2,1,0:T(8,128)S(1)}, f32[8,64,128]{2,1,0:T(8,128)S(1)}, u32[]{:S(2)}, u32[]{:S(2)}) collective-permute-start(f32[8,64,128]{2,1,0:T(8,128)S(1)} %multiply_add_fusion.2), channel_id=1, source_target_pairs={{0,8},{8,16},{16,24},{24,32},{32,40},{40,48},{48,56},{56,64},{64,7... | collective-permute-start | bytes 786440 | tf_op jit(solution)/shard_map/while/body/eval_jaxpr/ppermute | solution.py:12
  499.8 9.7 %collective-permute-start = (f32[8,64,128]{2,1,0:T(8,128)S(1)}, f32[8,64,128]{2,1,0:T(8,128)S(1)}, u32[]{:S(2)}, u32[]{:S(2)}) collective-permute-start(f32[8,64,128]{2,1,0:T(8,128)S(1)} %multiply_add_fusion.2), channel_id=1, source_target_pairs={{0,8},{8,16},{16,24},{24,32},{32,40},{40,48},{48,56},{56,64},{64,7... | collective-permute-start | bytes 786440 | tf_op jit(solution)/shard_map/while/body/eval_jaxpr/ppermute | solution.py:12
  509.7 10.5 %collective-permute-start = (f32[8,64,128]{2,1,0:T(8,128)S(1)}, f32[8,64,128]{2,1,0:T(8,128)S(1)}, u32[]{:S(2)}, u32[]{:S(2)}) collective-permute-start(f32[8,64,128]{2,1,0:T(8,128)S(1)} %multiply_add_fusion.2), channel_id=1, source_target_pairs={{0,8},{8,16},{16,24},{24,32},{32,40},{40,48},{48,56},{56,64},{64,7... | collective-permute-start | bytes 786440 | tf_op jit(solution)/shard_map/while/body/eval_jaxpr/ppermute | solution.py:12
  520.3 11.0 %collective-permute-start = (f32[8,64,128]{2,1,0:T(8,128)S(1)}, f32[8,64,128]{2,1,0:T(8,128)S(1)}, u32[]{:S(2)}, u32[]{:S(2)}) collective-permute-start(f32[8,64,128]{2,1,0:T(8,128)S(1)} %multiply_add_fusion.2), channel_id=1, source_target_pairs={{0,8},{8,16},{16,24},{24,32},{32,40},{40,48},{48,56},{56,64},{64,7... | collective-permute-start | bytes 786440 | tf_op jit(solution)/shard_map/while/body/eval_jaxpr/ppermute | solution.py:12
  531.5 12.9 %collective-permute-start = (f32[8,64,128]{2,1,0:T(8,128)S(1)}, f32[8,64,128]{2,1,0:T(8,128)S(1)}, u32[]{:S(2)}, u32[]{:S(2)}) collective-permute-start(f32[8,64,128]{2,1,0:T(8,128)S(1)} %multiply_add_fusion.2), channel_id=1, source_target_pairs={{0,8},{8,16},{16,24},{24,32},{32,40},{40,48},{48,56},{56,64},{64,7... | collective-permute-start | bytes 786440 | tf_op jit(solution)/shard_map/while/body/eval_jaxpr/ppermute | solution.py:12
  (20 other events, 433.9 us)
Sparse Core Ops, SparseCore 0:
  9.9 77.8 all-gather.5
  90.4 98.9 all-gather.3
  191.9 85.3 all-gather.7
  605.7 73.3 reduce-scatter.1
where the time goes:
time: 691 us; the launch traced here: 688 us
  waiting for transfers between devices  379 us (55%)
  starting transfers between devices  164 us (24%)
  blocking collectives  45.7 us (7%)
  local copies, waits for them, and re-layouts  42.3 us (6%)
  matrix products  27.4 us (4%)
  other arithmetic  14.1 us (2%)
  between operations  13.4 us (2%)
    ppermute x33, starting transfers between devices, passed_along(): return lax.ppermute(value, axis, pairs)  164 us
    ppermute x33, waiting for transfers between devices, passed_along(): return lax.ppermute(value, axis, pairs)  136 us
    all_gather x1, waiting for transfers between devices, local(): lax.all_gather(w_xz, 'seq', axis=0, tiled=True)  93.9 us
    all_gather x1, waiting for transfers between devices, local(): lax.all_gather(w_bc, 'seq', axis=0, tiled=True)  74.2 us
    reduce_scatter x1, waiting for transfers between devices, local(): lax.psum_scatter(partial_out, 'head', scatter_dimension=1, tiled=True)  73.5 us
    psum x1, blocking collectives, local(): total_sq = lax.psum(jnp.sum(gated * gated, axis=1), 'head')  45.7 us
    dynamic_update_slice x4, local copies, waits for them, and re-layouts, local(): local_state, parts = lax.scan(block_step, jnp.zeros_like(state_in), inputs)  24.1 us
  transfers between devices with their start and end apart: 37, of which 36 were waited for; matrix products, arithmetic and copies ran while one was open for 11% of the time, Pallas kernels for 0%

commit v1 on v0

--- a/solution.py
+++ b/solution.py
@@ -4,6 +4,14 @@
 from jax.sharding import PartitionSpec as P
 
 Q = 256
+
+
+def gather_by_exchange(shard, axis, dim):
+    size = lax.axis_size(axis)
+    repeats = [size if d == dim else 1 for d in range(shard.ndim)]
+    return lax.all_to_all(
+        jnp.tile(shard, repeats), axis, split_axis=dim, concat_axis=dim, tiled=True
+    )
 
 
 def passed_along(value, axis, by):
@@ -63,10 +71,7 @@
     inner = heads * head_dim
     seq_count = lax.axis_size("seq")
     first = lax.axis_index("seq") == 0
-    pieces = (
-        lax.all_gather(w_xz, "seq", axis=0, tiled=True),
-        lax.all_gather(w_bc, "seq", axis=0, tiled=True),
-    )
+    pieces = (lax.all_gather(w_xz, "seq", axis=0, tiled=True), gather_by_exchange(w_bc, "seq", 0))
     count = pieces[0].shape[0]
     xz = jnp.dot(tokens, pieces[0].reshape(count, 2 * inner), preferred_element_type=jnp.float32)
     bc_sum = jnp.dot(tokens, pieces[1], preferred_element_type=jnp.float32)

time: 691 us -> 634 us (0.918)
  waiting for transfers between devices: 379 us -> 304 us
  starting transfers between devices: 164 us -> 182 us
    all_gather x1 -> x0, waiting for transfers between devices: 74.2 us -> none  [local(): lax.all_gather(w_bc, 'seq', axis=0, tiled=True)]
    all_to_all x0 -> x1, waiting for transfers between devices: none -> 56.6 us  [gather_by_exchange(): lax.all_to_all(jnp.tile(shard, repeats), axis, split_axis=dim, concat_axi...]
    all_gather x1, waiting for transfers between devices: 93.9 us -> 40.1 us  [local(): lax.all_gather(w_xz, 'seq', axis=0, tiled=True)]
    all_to_all x0 -> x1, starting transfers between devices: none -> 12 us  [gather_by_exchange(): lax.all_to_all(jnp.tile(shard, repeats), axis, split_axis=dim, concat_axi...]
  transfers between devices with their start and end apart: 37 -> 37, of which waited for: 36 -> 36; matrix products, arithmetic and copies ran while one was open for 11% -> 12% of each run, Pallas kernels for 0% -> 0%
where the time goes in v1:
time: 634 us; the launch traced here: 632 us
  waiting for transfers between devices  304 us (48%)
  starting transfers between devices  182 us (29%)
  blocking collectives  45.8 us (7%)
  local copies, waits for them, and re-layouts  45.2 us (7%)
  matrix products  26.9 us (4%)
  between operations  13.4 us (2%)
  other arithmetic  12.5 us (2%)
    ppermute x33, starting transfers between devices, passed_along(): return lax.ppermute(value, axis, pairs)  170 us
    ppermute x33, waiting for transfers between devices, passed_along(): return lax.ppermute(value, axis, pairs)  130 us
    reduce_scatter x1, waiting for transfers between devices, local(): lax.psum_scatter(partial_out, 'head', scatter_dimension=1, tiled=True)  76.3 us
    all_to_all x1, waiting for transfers between devices, gather_by_exchange(): lax.all_to_all(jnp.tile(shard, repeats), axis, split_axis=dim, concat_axi...  56.6 us
    psum x1, blocking collectives, local(): total_sq = lax.psum(jnp.sum(gated * gated, axis=1), 'head')  45.8 us
    all_gather x1, waiting for transfers between devices, local(): lax.all_gather(w_xz, 'seq', axis=0, tiled=True)  40.1 us
    dynamic_update_slice x4, local copies, waits for them, and re-layouts, local(): local_state, parts = lax.scan(block_step, jnp.zeros_like(state_in), inputs)  24.1 us
  transfers between devices with their start and end apart: 37, of which 36 were waited for; matrix products, arithmetic and copies ran while one was open for 12% of the time, Pallas kernels for 0%

profile of v1, /device:TPU:1, one launch (start us, length us, event | category | flops | bytes accessed | tf_op | source)
XLA Modules:
  0.0 631.5 jit_solution(11345245610435511484)
XLA Ops:
  9.7 12.0 %all-to-all-start = ((bf16[32,128,256]{2,1,0:T(8,128)(2,1)}), bf16[32,128,256]{2,1,0:T(8,128)(2,1)S(1)}, u32[]{:S(2)}, u32[]{:S(2)}) async-start(bf16[32,128,256]{2,1,0:T(8,128)(2,1)} %tile.2), calls=%async_computation | async-start | bytes 4194304 | tf_op jit(solution)/shard_map/all_to_all | solution.py:12
  24.1 56.6 %all-to-all-done = bf16[32,128,256]{2,1,0:T(8,128)(2,1)S(1)} async-done(((bf16[32,128,256]{2,1,0:T(8,128)(2,1)}), bf16[32,128,256]{2,1,0:T(8,128)(2,1)S(1)}, u32[]{:S(2)}, u32[]{:S(2)}) %all-to-all-start) | async-done | bytes 2097184 | tf_op jit(solution)/shard_map/all_to_all | solution.py:12
  89.5 40.1 %all-gather.3.cloned.1.call-done = bf16[4096,2,512]{2,1,0:T(2,128)(2,1)} async-done(((bf16[128,2,512]{2,1,0:T(2,128)(2,1)}), bf16[4096,2,512]{2,1,0:T(2,128)(2,1)}) %all-gather.3.cloned.1.call-update) | async-done | bytes 8388624 | tf_op jit(solution)/shard_map/all_gather | solution.py:74
  129.6 9.3 %copy.40 = bf16[512,8,2,512]{3,1,2,0:T(8,128)(2,1)} copy(bf16[512,8,2,512]{3,2,1,0:T(2,128)(2,1)} %bitcast.89) | data formatting | bytes 16777216
  138.9 9.3 %convolution_convert_fusion = bf16[512,1024]{1,0:T(8,128)(2,1)S(1)} fusion(bf16[512,4096]{1,0:T(8,128)(2,1)} %param.16, bf16[4096,1024]{1,0:T(8,128)(2,1)} %bitcast.90), kind=kOutput, calls=%fused_computation.44 | convolution fusion | flops 4295491584 | bytes 13631488 | tf_op jit(solution)/shard_map/dot_general | solution.py:76
  154.4 30.3 %while.24 = (s32[]{:T(128)}, f32[8,64,128]{2,1,0:T(8,128)S(1)}, f32[2,256,8,64]{1,0,3,2:T(2,128)}, f32[2,256,8]{1,2,0:T(8,128)S(1)}, bf16[2,256,8,64]{1,3,2,0:T(...) while((s32[]{:T(128)}, f32[8,64,128]{2,1,0:T(8,128)S(1)}, ...), condition=%wide.region_3.4_spmd.clone, body=%wide.region_0.3_spmd.clone.sunk | while | flops 322801696 | bytes 6277456 | solution.py:97
  157.5 11.5 %dynamic_update_slice.6 = f32[2,256,8,64]{1,0,3,2:T(2,128)} dynamic-update-slice(f32[2,256,8,64]{1,0,3,2:T(2,128)} %get-tuple-element.276, f32[1,256,8,64]{1,0,3,2:T(1,128)S(1)} %copy.42, s32[]{:T(128)} %get-tuple-element.274, s32[]{:T(128)} %constant.46.clone.1..sunk, s32[]{:T(128)} %constant.46.clone.1..sunk, s32[]{:T(128)} %constant.46.clone.1..sunk) | dynamic-update-slice | bytes 1048580 | tf_op jit(solution)/shard_map/while/body/jit(dynamic_update_index_in_dim)/dynamic_update_slice | solution.py:97
  172.7 11.5 %dynamic_update_slice.6 = f32[2,256,8,64]{1,0,3,2:T(2,128)} dynamic-update-slice(f32[2,256,8,64]{1,0,3,2:T(2,128)} %get-tuple-element.276, f32[1,256,8,64]{1,0,3,2:T(1,128)S(1)} %copy.42, s32[]{:T(128)} %get-tuple-element.274, s32[]{:T(128)} %constant.46.clone.1..sunk, s32[]{:T(128)} %constant.46.clone.1..sunk, s32[]{:T(128)} %constant.46.clone.1..sunk) | dynamic-update-slice | bytes 1048580 | tf_op jit(solution)/shard_map/while/body/jit(dynamic_update_index_in_dim)/dynamic_update_slice | solution.py:97
  186.9 298.5 %while.23 = (s32[]{:T(128)}, f32[8,64,128]{2,1,0:T(8,128)S(1)}, pred[]{:T(512)}, f32[8]{0:T(128)S(1)}, f32[8,64,128]{2,1,0:T(8,128)S(1)}, /*index=5*/f32[8,64,128]{2,1,0:T(8,128)S(1)}, s32[]{:T(128)}) while((s32[]{:T(128)}, f32[8,64,128]{2,1,0:T(8,128)S(1)}, pred[]{:T(512)}, f32[8]{0:T(128)S(1)}, f32[8,64,128]{2,1,0:T(8,128)S(1)}, ...), condition=%wide.region_7.8_spmd, body=%wide.region_6.7_spmd.sunk | while | flops 196610 | bytes 2621590 | solution.py:108
  190.8 8.8 %collective-permute-done = f32[8,64,128]{2,1,0:T(8,128)S(1)} collective-permute-done((f32[8,64,128]{2,1,0:T(8,128)S(1)}, f32[8,64,128]{2,1,0:T(8,128)S(1)}, u32[]{:S(2)}, u32[]{:S(2)}) %collective-permute-start) | collective-permute-done | bytes 262176 | tf_op jit(solution)/shard_map/while/body/eval_jaxpr/ppermute | solution.py:20
  209.1 6.0 collective-permute-start
  279.5 6.0 collective-permute-start
  297.9 7.5 %collective-permute-start = (f32[8,64,128]{2,1,0:T(8,128)S(1)}, f32[8,64,128]{2,1,0:T(8,128)S(1)}, u32[]{:S(2)}, u32[]{:S(2)}) collective-permute-start(f32[8,64,128]{2,1,0:T(8,128)S(1)} %multiply_add_fusion.2), channel_id=1, source_target_pairs={{0,8},{8,16},{16,24},{24,32},{32,40},{40,48},{48,56},{56,64},{64,7... | collective-permute-start | bytes 786440 | tf_op jit(solution)/shard_map/while/body/eval_jaxpr/ppermute | solution.py:20
  353.7 5.6 collective-permute-start
  370.4 5.7 collective-permute-done
  403.2 6.3 %collective-permute-start = (f32[8,64,128]{2,1,0:T(8,128)S(1)}, f32[8,64,128]{2,1,0:T(8,128)S(1)}, u32[]{:S(2)}, u32[]{:S(2)}) collective-permute-start(f32[8,64,128]{2,1,0:T(8,128)S(1)} %multiply_add_fusion.2), channel_id=1, source_target_pairs={{0,8},{8,16},{16,24},{24,32},{32,40},{40,48},{48,56},{56,64},{64,7... | collective-permute-start | bytes 786440 | tf_op jit(solution)/shard_map/while/body/eval_jaxpr/ppermute | solution.py:20
  413.0 9.1 %collective-permute-start = (f32[8,64,128]{2,1,0:T(8,128)S(1)}, f32[8,64,128]{2,1,0:T(8,128)S(1)}, u32[]{:S(2)}, u32[]{:S(2)}) collective-permute-start(f32[8,64,128]{2,1,0:T(8,128)S(1)} %multiply_add_fusion.2), channel_id=1, source_target_pairs={{0,8},{8,16},{16,24},{24,32},{32,40},{40,48},{48,56},{56,64},{64,7... | collective-permute-start | bytes 786440 | tf_op jit(solution)/shard_map/while/body/eval_jaxpr/ppermute | solution.py:20
  442.5 6.2 collective-permute-start
  452.2 6.2 collective-permute-start
  462.3 6.2 collective-permute-start
  473.2 6.5 %collective-permute-start = (f32[8,64,128]{2,1,0:T(8,128)S(1)}, f32[8,64,128]{2,1,0:T(8,128)S(1)}, u32[]{:S(2)}, u32[]{:S(2)}) collective-permute-start(f32[8,64,128]{2,1,0:T(8,128)S(1)} %multiply_add_fusion.2), channel_id=1, source_target_pairs={{0,8},{8,16},{16,24},{24,32},{32,40},{40,48},{48,56},{56,64},{64,7... | collective-permute-start | bytes 786440 | tf_op jit(solution)/shard_map/while/body/eval_jaxpr/ppermute | solution.py:20
  493.0 45.8 %psum.7 = f32[512]{0:T(512)S(1)} all-reduce(f32[512]{0:T(512)S(1)} %get-tuple-element.160), channel_id=1, replica_groups=mesh['seq'=32,'head'=8] {'head'}, use_global_device_ids=true, to_apply=%region_9.10 | all-reduce | flops 512 | bytes 4096 | tf_op jit(solution)/shard_map/psum | solution.py:115
  538.8 7.8 %fusion.38 = f32[512,4096]{1,0:T(8,128)} fusion(bf16[512,4096]{1,0:T(8,128)(2,1)} %all-gather.5.cloned.1.call-done, f32[512,512]{1,0:T(8,128)S(1)} %get-tuple-element.161, f32[512]{0:T(512)S(1)} %copy-done.3, f32[512]{0:T(512)S(1)} %add_rsqrt_fusion), kind=kOutput, calls=%fused_computation.66 | convolution fusion | flops 2148270080 | bytes 13635584 | tf_op jit(solution)/shard_map/dot_general | solution.py:118
  546.6 76.3 %reduce-scatter.2.cloned.1.call-done = f32[512,512]{1,0:T(8,128)} async-done(((f32[512,4096]{1,0:T(8,128)}), f32[512,512]{1,0:T(8,128)}) %reduce-scatter.2.cloned.1.call-update) | async-done | bytes 1048592 | tf_op jit(solution)/shard_map/reduce_scatter | solution.py:121
  (209 shorter events, 256.6 us)
Async XLA Ops:
  6.5 123.1 %all-gather.3.cloned.1.call-start = ((), (), s32[]{:S(2)}) async-start(), calls=%async_computation.2 | async-start | bytes 8650752 | tf_op jit(solution)/shard_map/all_gather | solution.py:74
  9.7 71.0 %all-to-all-start = ((bf16[32,128,256]{2,1,0:T(8,128)(2,1)}), bf16[32,128,256]{2,1,0:T(8,128)(2,1)S(1)}, u32[]{:S(2)}, u32[]{:S(2)}) async-start(bf16[32,128,256]{2,1,0:T(8,128)(2,1)} %tile.2), calls=%async_computation | async-start | bytes 4194304 | tf_op jit(solution)/shard_map/all_to_all | solution.py:12
  21.7 517.0 %all-gather.5.cloned.1.call-start = ((), (), s32[]{:S(2)}) async-start(), calls=%async_computation.3 | async-start | bytes 4325376 | tf_op jit(solution)/shard_map/all_gather | solution.py:119
  22.5 600.4 %reduce-scatter.2.cloned.1.call-start = ((), (), s32[]{:S(2)}) async-start(), calls=%async_computation.4 | async-start | bytes 9437184 | tf_op jit(solution)/shard_map/reduce_scatter | solution.py:121
  187.0 12.6 %collective-permute-start = (f32[8,64,128]{2,1,0:T(8,128)S(1)}, f32[8,64,128]{2,1,0:T(8,128)S(1)}, u32[]{:S(2)}, u32[]{:S(2)}) collective-permute-start(f32[8,64,128]{2,1,0:T(8,128)S(1)} %multiply_add_fusion.2), channel_id=1, source_target_pairs={{0,8},{8,16},{16,24},{24,32},{32,40},{40,48},{48,56},{56,64},{64,7... | collective-permute-start | bytes 786440 | tf_op jit(solution)/shard_map/while/body/eval_jaxpr/ppermute | solution.py:20
  199.7 9.2 %collective-permute-start = (f32[8,64,128]{2,1,0:T(8,128)S(1)}, f32[8,64,128]{2,1,0:T(8,128)S(1)}, u32[]{:S(2)}, u32[]{:S(2)}) collective-permute-start(f32[8,64,128]{2,1,0:T(8,128)S(1)} %multiply_add_fusion.2), channel_id=1, source_target_pairs={{0,8},{8,16},{16,24},{24,32},{32,40},{40,48},{48,56},{56,64},{64,7... | collective-permute-start | bytes 786440 | tf_op jit(solution)/shard_map/while/body/eval_jaxpr/ppermute | solution.py:20
  209.1 10.3 %collective-permute-start = (f32[8,64,128]{2,1,0:T(8,128)S(1)}, f32[8,64,128]{2,1,0:T(8,128)S(1)}, u32[]{:S(2)}, u32[]{:S(2)}) collective-permute-start(f32[8,64,128]{2,1,0:T(8,128)S(1)} %multiply_add_fusion.2), channel_id=1, source_target_pairs={{0,8},{8,16},{16,24},{24,32},{32,40},{40,48},{48,56},{56,64},{64,7... | collective-permute-start | bytes 786440 | tf_op jit(solution)/shard_map/while/body/eval_jaxpr/ppermute | solution.py:20
  227.9 9.3 %collective-permute-start = (f32[8,64,128]{2,1,0:T(8,128)S(1)}, f32[8,64,128]{2,1,0:T(8,128)S(1)}, u32[]{:S(2)}, u32[]{:S(2)}) collective-permute-start(f32[8,64,128]{2,1,0:T(8,128)S(1)} %multiply_add_fusion.2), channel_id=1, source_target_pairs={{0,8},{8,16},{16,24},{24,32},{32,40},{40,48},{48,56},{56,64},{64,7... | collective-permute-start | bytes 786440 | tf_op jit(solution)/shard_map/while/body/eval_jaxpr/ppermute | solution.py:20
  237.4 9.4 %collective-permute-start = (f32[8,64,128]{2,1,0:T(8,128)S(1)}, f32[8,64,128]{2,1,0:T(8,128)S(1)}, u32[]{:S(2)}, u32[]{:S(2)}) collective-permute-start(f32[8,64,128]{2,1,0:T(8,128)S(1)} %multiply_add_fusion.2), channel_id=1, source_target_pairs={{0,8},{8,16},{16,24},{24,32},{32,40},{40,48},{48,56},{56,64},{64,7... | collective-permute-start | bytes 786440 | tf_op jit(solution)/shard_map/while/body/eval_jaxpr/ppermute | solution.py:20
  246.9 8.7 %collective-permute-start = (f32[8,64,128]{2,1,0:T(8,128)S(1)}, f32[8,64,128]{2,1,0:T(8,128)S(1)}, u32[]{:S(2)}, u32[]{:S(2)}) collective-permute-start(f32[8,64,128]{2,1,0:T(8,128)S(1)} %multiply_add_fusion.2), channel_id=1, source_target_pairs={{0,8},{8,16},{16,24},{24,32},{32,40},{40,48},{48,56},{56,64},{64,7... | collective-permute-start | bytes 786440 | tf_op jit(solution)/shard_map/while/body/eval_jaxpr/ppermute | solution.py:20
  279.5 9.3 %collective-permute-start = (f32[8,64,128]{2,1,0:T(8,128)S(1)}, f32[8,64,128]{2,1,0:T(8,128)S(1)}, u32[]{:S(2)}, u32[]{:S(2)}) collective-permute-start(f32[8,64,128]{2,1,0:T(8,128)S(1)} %multiply_add_fusion.2), channel_id=1, source_target_pairs={{0,8},{8,16},{16,24},{24,32},{32,40},{40,48},{48,56},{56,64},{64,7... | collective-permute-start | bytes 786440 | tf_op jit(solution)/shard_map/while/body/eval_jaxpr/ppermute | solution.py:20
  288.9 8.8 %collective-permute-start = (f32[8,64,128]{2,1,0:T(8,128)S(1)}, f32[8,64,128]{2,1,0:T(8,128)S(1)}, u32[]{:S(2)}, u32[]{:S(2)}) collective-permute-start(f32[8,64,128]{2,1,0:T(8,128)S(1)} %multiply_add_fusion.2), channel_id=1, source_target_pairs={{0,8},{8,16},{16,24},{24,32},{32,40},{40,48},{48,56},{56,64},{64,7... | collective-permute-start | bytes 786440 | tf_op jit(solution)/shard_map/while/body/eval_jaxpr/ppermute | solution.py:20
  297.9 10.7 %collective-permute-start = (f32[8,64,128]{2,1,0:T(8,128)S(1)}, f32[8,64,128]{2,1,0:T(8,128)S(1)}, u32[]{:S(2)}, u32[]{:S(2)}) collective-permute-start(f32[8,64,128]{2,1,0:T(8,128)S(1)} %multiply_add_fusion.2), channel_id=1, source_target_pairs={{0,8},{8,16},{16,24},{24,32},{32,40},{40,48},{48,56},{56,64},{64,7... | collective-permute-start | bytes 786440 | tf_op jit(solution)/shard_map/while/body/eval_jaxpr/ppermute | solution.py:20
  343.7 9.8 %collective-permute-start = (f32[8,64,128]{2,1,0:T(8,128)S(1)}, f32[8,64,128]{2,1,0:T(8,128)S(1)}, u32[]{:S(2)}, u32[]{:S(2)}) collective-permute-start(f32[8,64,128]{2,1,0:T(8,128)S(1)} %multiply_add_fusion.2), channel_id=1, source_target_pairs={{0,8},{8,16},{16,24},{24,32},{32,40},{40,48},{48,56},{56,64},{64,7... | collective-permute-start | bytes 786440 | tf_op jit(solution)/shard_map/while/body/eval_jaxpr/ppermute | solution.py:20
  353.7 11.3 %collective-permute-start = (f32[8,64,128]{2,1,0:T(8,128)S(1)}, f32[8,64,128]{2,1,0:T(8,128)S(1)}, u32[]{:S(2)}, u32[]{:S(2)}) collective-permute-start(f32[8,64,128]{2,1,0:T(8,128)S(1)} %multiply_add_fusion.2), channel_id=1, source_target_pairs={{0,8},{8,16},{16,24},{24,32},{32,40},{40,48},{48,56},{56,64},{64,7... | collective-permute-start | bytes 786440 | tf_op jit(solution)/shard_map/while/body/eval_jaxpr/ppermute | solution.py:20
  365.1 11.0 %collective-permute-start = (f32[8,64,128]{2,1,0:T(8,128)S(1)}, f32[8,64,128]{2,1,0:T(8,128)S(1)}, u32[]{:S(2)}, u32[]{:S(2)}) collective-permute-start(f32[8,64,128]{2,1,0:T(8,128)S(1)} %multiply_add_fusion.2), channel_id=1, source_target_pairs={{0,8},{8,16},{16,24},{24,32},{32,40},{40,48},{48,56},{56,64},{64,7... | collective-permute-start | bytes 786440 | tf_op jit(solution)/shard_map/while/body/eval_jaxpr/ppermute | solution.py:20
  376.3 9.9 %collective-permute-start = (f32[8,64,128]{2,1,0:T(8,128)S(1)}, f32[8,64,128]{2,1,0:T(8,128)S(1)}, u32[]{:S(2)}, u32[]{:S(2)}) collective-permute-start(f32[8,64,128]{2,1,0:T(8,128)S(1)} %multiply_add_fusion.2), channel_id=1, source_target_pairs={{0,8},{8,16},{16,24},{24,32},{32,40},{40,48},{48,56},{56,64},{64,7... | collective-permute-start | bytes 786440 | tf_op jit(solution)/shard_map/while/body/eval_jaxpr/ppermute | solution.py:20
  386.3 8.6 %collective-permute-start = (f32[8,64,128]{2,1,0:T(8,128)S(1)}, f32[8,64,128]{2,1,0:T(8,128)S(1)}, u32[]{:S(2)}, u32[]{:S(2)}) collective-permute-start(f32[8,64,128]{2,1,0:T(8,128)S(1)} %multiply_add_fusion.2), channel_id=1, source_target_pairs={{0,8},{8,16},{16,24},{24,32},{32,40},{40,48},{48,56},{56,64},{64,7... | collective-permute-start | bytes 786440 | tf_op jit(solution)/shard_map/while/body/eval_jaxpr/ppermute | solution.py:20
  403.2 9.6 %collective-permute-start = (f32[8,64,128]{2,1,0:T(8,128)S(1)}, f32[8,64,128]{2,1,0:T(8,128)S(1)}, u32[]{:S(2)}, u32[]{:S(2)}) collective-permute-start(f32[8,64,128]{2,1,0:T(8,128)S(1)} %multiply_add_fusion.2), channel_id=1, source_target_pairs={{0,8},{8,16},{16,24},{24,32},{32,40},{40,48},{48,56},{56,64},{64,7... | collective-permute-start | bytes 786440 | tf_op jit(solution)/shard_map/while/body/eval_jaxpr/ppermute | solution.py:20
  413.0 12.4 %collective-permute-start = (f32[8,64,128]{2,1,0:T(8,128)S(1)}, f32[8,64,128]{2,1,0:T(8,128)S(1)}, u32[]{:S(2)}, u32[]{:S(2)}) collective-permute-start(f32[8,64,128]{2,1,0:T(8,128)S(1)} %multiply_add_fusion.2), channel_id=1, source_target_pairs={{0,8},{8,16},{16,24},{24,32},{32,40},{40,48},{48,56},{56,64},{64,7... | collective-permute-start | bytes 786440 | tf_op jit(solution)/shard_map/while/body/eval_jaxpr/ppermute | solution.py:20
  442.5 9.5 %collective-permute-start = (f32[8,64,128]{2,1,0:T(8,128)S(1)}, f32[8,64,128]{2,1,0:T(8,128)S(1)}, u32[]{:S(2)}, u32[]{:S(2)}) collective-permute-start(f32[8,64,128]{2,1,0:T(8,128)S(1)} %multiply_add_fusion.2), channel_id=1, source_target_pairs={{0,8},{8,16},{16,24},{24,32},{32,40},{40,48},{48,56},{56,64},{64,7... | collective-permute-start | bytes 786440 | tf_op jit(solution)/shard_map/while/body/eval_jaxpr/ppermute | solution.py:20
  452.2 10.0 %collective-permute-start = (f32[8,64,128]{2,1,0:T(8,128)S(1)}, f32[8,64,128]{2,1,0:T(8,128)S(1)}, u32[]{:S(2)}, u32[]{:S(2)}) collective-permute-start(f32[8,64,128]{2,1,0:T(8,128)S(1)} %multiply_add_fusion.2), channel_id=1, source_target_pairs={{0,8},{8,16},{16,24},{24,32},{32,40},{40,48},{48,56},{56,64},{64,7... | collective-permute-start | bytes 786440 | tf_op jit(solution)/shard_map/while/body/eval_jaxpr/ppermute | solution.py:20
  462.3 10.7 %collective-permute-start = (f32[8,64,128]{2,1,0:T(8,128)S(1)}, f32[8,64,128]{2,1,0:T(8,128)S(1)}, u32[]{:S(2)}, u32[]{:S(2)}) collective-permute-start(f32[8,64,128]{2,1,0:T(8,128)S(1)} %multiply_add_fusion.2), channel_id=1, source_target_pairs={{0,8},{8,16},{16,24},{24,32},{32,40},{40,48},{48,56},{56,64},{64,7... | collective-permute-start | bytes 786440 | tf_op jit(solution)/shard_map/while/body/eval_jaxpr/ppermute | solution.py:20
  473.2 12.1 %collective-permute-start = (f32[8,64,128]{2,1,0:T(8,128)S(1)}, f32[8,64,128]{2,1,0:T(8,128)S(1)}, u32[]{:S(2)}, u32[]{:S(2)}) collective-permute-start(f32[8,64,128]{2,1,0:T(8,128)S(1)} %multiply_add_fusion.2), channel_id=1, source_target_pairs={{0,8},{8,16},{16,24},{24,32},{32,40},{40,48},{48,56},{56,64},{64,7... | collective-permute-start | bytes 786440 | tf_op jit(solution)/shard_map/while/body/eval_jaxpr/ppermute | solution.py:20
  (23 other events, 291.4 us)
Sparse Core Ops, SparseCore 0:
  9.9 119.6 all-gather.2
  132.1 85.2 all-gather.4
  546.7 76.1 reduce-scatter.1
